TPU v7x, 256 devices: a whole 4x4x8 slice. The times are simulated.
256 devices in a mesh: rep: 16 (over x, y_hi, core), hid: 16 (over y_lo, z).
Axes of the slice: x: 4, y: 4 (y_hi: 2, y_lo: 2; y = y_hi * 2 + y_lo), z: 8, core: 2. Of those that a mesh axis runs over, the one named last changes fastest.
Arguments:
- tokens: bfloat16 [2, 8192, 1152], P(None, ('rep', 'hid')), may hold values from -6 to 6
- targets: bfloat16 [2, 8192, 1152], P(None, ('rep', 'hid')), may hold values from -6 to 6
- w_gate: float32 [16, 6912, 1152], P('rep', 'hid'), may hold values from -6 to 6
- w_up: float32 [16, 6912, 1152], P('rep', 'hid'), may hold values from -6 to 6
- w_down: float32 [16, 6912, 1152], P('rep', 'hid'), may hold values from -6 to 6
Outputs:
- new_gate: float32 [16, 6912, 1152], P('rep', 'hid')
- new_up: float32 [16, 6912, 1152], P('rep', 'hid')
- new_down: float32 [16, 6912, 1152], P('rep', 'hid')
All inputs are finite; a program needn't handle non-finite values.
Results may differ from a plain program's by a relative error of at most 0.0086.
Values may be sent and summed in bfloat16 or wider, within the bound.
No kernel may reach another device: no remote copies, remote signals or barrier semaphores. Data moves between devices by JAX's collectives and lax.ppermute only.
A program may use at most 128 MiB of HBM per device.

v0:
```python
import jax
import jax.numpy as jnp
from jax import lax
from jax.sharding import PartitionSpec as P

D = 1152
FF = 6912
STEPS = 2
LEARNING_RATE = 0.5


def swapped(value, axis, distance):
    mask = 2**distance
    pairs = [(source, source ^ mask) for source in range(lax.axis_size(axis))]
    return lax.ppermute(value, axis, pairs)


def gelu_tanh(value):
    return jax.nn.gelu(value, approximate=True)


def contract_cols(left, right):
    return lax.dot_general(
        left, right, (((1,), (1,)), ((), ())), preferred_element_type=jnp.float32
    )


def contract_rows(left, right):
    return lax.dot_general(
        left, right, (((0,), (0,)), ((), ())), preferred_element_type=jnp.float32
    )


def local(tokens, targets, w_gate, w_up, w_down):
    scale_model = float(D) ** (-0.5)
    scale_hidden = float(FF) ** (-0.5)
    all_tokens, all_targets = (
        lax.all_gather(tokens, "hid", axis=1, tiled=True),
        lax.all_gather(targets, "hid", axis=1, tiled=True),
    )
    weights = (w_gate[0], w_up[0], w_down[0])
    for step_index in range(STEPS):
        token_batch = all_tokens[step_index]
        gate_half = weights[0].astype(jnp.bfloat16)
        up_half = weights[1].astype(jnp.bfloat16)
        down_half = weights[2].astype(jnp.bfloat16)
        gate_value = contract_cols(token_batch, gate_half) * scale_model
        up_value = contract_cols(token_batch, up_half) * scale_model
        activated, gelu_back = jax.vjp(gelu_tanh, gate_value)
        hidden = (activated * up_value).astype(jnp.bfloat16)
        partial_out = jnp.dot(hidden, down_half, preferred_element_type=jnp.float32) * scale_hidden
        output = lax.psum(partial_out, "hid")
        residual = (output - all_targets[step_index].astype(jnp.float32)).astype(jnp.bfloat16)
        grad_down = contract_rows(hidden, residual) * scale_hidden
        hidden_grad = contract_cols(residual, down_half) * scale_hidden
        gate_grad = gelu_back(hidden_grad * up_value)[0].astype(jnp.bfloat16)
        up_grad = (hidden_grad * activated).astype(jnp.bfloat16)
        grad_gate = contract_rows(gate_grad, token_batch) * scale_model
        grad_up = contract_rows(up_grad, token_batch) * scale_model
        gradients = (grad_gate, grad_up, grad_down)
        stepped = tuple(
            (weight - LEARNING_RATE * gradient for weight, gradient in zip(weights, gradients))
        )
        partner_new = swapped(stepped, "rep", step_index)
        weights = tuple(((mine + theirs) * 0.5 for mine, theirs in zip(stepped, partner_new)))
    return (weights[0][None], weights[1][None], weights[2][None])


def solution(mesh):
    placed = (
        P(None, ("rep", "hid"), None),
        P(None, ("rep", "hid"), None),
        P("rep", "hid", None),
        P("rep", "hid", None),
        P("rep", "hid", None),
    )
    return jax.shard_map(
        local,
        mesh=mesh,
        in_specs=placed,
        out_specs=(P("rep", "hid", None), P("rep", "hid", None), P("rep", "hid", None)),
        check_vma=False,
    )
```

profile of v0, /device:TPU:2, one launch (start us, length us, event | category | flops | bytes accessed | tf_op | source)
XLA Modules:
  0.0 596.4 jit_solution(7558475511796509803)
XLA Ops:
  8.7 76.2 %all-gather.3.cloned.1.call-done = bf16[2,512,1152]{2,1,0:T(8,128)(2,1)} async-done(((bf16[2,32,1152]{2,1,0:T(8,128)(2,1)}), bf16[2,512,1152]{2,1,0:T(8,128)(2,1)}) %all-gather.3.cloned.1.call-update) | async-done | bytes 2359312 | tf_op jit(solution)/shard_map/all_gather | solution.py:38
  84.9 2.8 convolution_multiply_fusion.13
  87.7 3.5 multiply_convert_fusion.3
  92.0 2.3 convolution_multiply_fusion.1
  94.4 61.8 %all-gather.5.cloned.1.call-done = bf16[2,512,1152]{2,1,0:T(8,128)(2,1)} async-done(((bf16[2,32,1152]{2,1,0:T(8,128)(2,1)}), bf16[2,512,1152]{2,1,0:T(8,128)(2,1)}) %all-gather.5.cloned.1.call-update) | async-done | bytes 2359312 | tf_op jit(solution)/shard_map/all_gather | solution.py:39
  156.2 143.4 %all-reduce.3.cloned.1.call-done = f32[512,1152]{1,0:T(8,128)} async-done(((f32[512,1152]{1,0:T(8,128)}), f32[512,1152]{1,0:T(8,128)}) %all-reduce.3.cloned.1.call-update) | async-done | bytes 2359312 | tf_op jit(solution)/shard_map/psum | solution.py:52
  299.6 3.5 convolution_multiply_fusion.11
  303.2 1.3 fusion.5
  305.4 1.4 copy-done.9
  306.9 0.9 fusion.3
  307.9 1.0 fusion.4
  309.4 0.8 fusion.9
  310.8 1.1 collective-permute-done.2
  312.2 1.1 copy-done.16
  313.2 1.5 collective-permute-done.1
  314.7 1.9 multiply_convert_fusion.1
  316.6 0.8 copy-done.20
  317.4 2.3 convolution_multiply_fusion
  319.7 140.9 %all-reduce.5.cloned.1.call-done = f32[512,1152]{1,0:T(8,128)} async-done(((f32[512,1152]{1,0:T(8,128)}), f32[512,1152]{1,0:T(8,128)}) %all-reduce.5.cloned.1.call-update) | async-done | bytes 2359312 | tf_op jit(solution)/shard_map/psum | solution.py:52
  460.6 3.2 convolution_multiply_fusion.8
  464.2 1.0 fusion.1
  465.2 3.5 collective-permute-start.4
  468.7 1.4 fusion.2
  470.1 1.1 collective-permute-start.3
  472.2 0.9 fusion
  473.1 1.6 collective-permute-start.5
  474.7 38.5 %collective-permute-done.4 = f32[432,1152]{1,0:T(8,128)S(1)} collective-permute-done((f32[432,1152]{1,0:T(8,128)S(1)}, f32[432,1152]{1,0:T(8,128)S(1)}, u32[]{:S(2)}, u32[]{:S(2)}) %collective-permute-start.4) | collective-permute-done | bytes 1990688 | tf_op jit(solution)/shard_map/ppermute | solution.py:15
  513.2 1.6 multiply_bitcast_fusion.1
  514.7 41.1 %collective-permute-done.3 = f32[432,1152]{1,0:T(8,128)S(1)} collective-permute-done((f32[432,1152]{1,0:T(8,128)S(1)}, f32[432,1152]{1,0:T(8,128)S(1)}, u32[]{:S(2)}, u32[]{:S(2)}) %collective-permute-start.3) | collective-permute-done | bytes 1990688 | tf_op jit(solution)/shard_map/ppermute | solution.py:15
  555.8 1.6 multiply_bitcast_fusion.2
  557.4 31.0 %collective-permute-done.5 = f32[432,1152]{1,0:T(8,128)S(1)} collective-permute-done((f32[432,1152]{1,0:T(8,128)S(1)}, f32[432,1152]{1,0:T(8,128)S(1)}, u32[]{:S(2)}, u32[]{:S(2)}) %collective-permute-start.5) | collective-permute-done | bytes 1990688 | tf_op jit(solution)/shard_map/ppermute | solution.py:15
  588.4 1.6 multiply_bitcast_fusion
  (66 shorter events, 6.2 us)
Async XLA Ops:
  7.2 77.7 %all-gather.3.cloned.1.call-start = ((), (), s32[]{:S(2)}) async-start(), calls=%async_computation | async-start | bytes 2506752 | tf_op jit(solution)/shard_map/all_gather | solution.py:38
  7.9 148.3 %all-gather.5.cloned.1.call-start = ((), (), s32[]{:S(2)}) async-start(), calls=%async_computation.2 | async-start | bytes 2506752 | tf_op jit(solution)/shard_map/all_gather | solution.py:39
  8.6 290.9 %all-reduce.3.cloned.1.call-start = ((), (), s32[]{:S(2)}) async-start(), calls=%async_computation.1 | async-start | bytes 4718592 | tf_op jit(solution)/shard_map/psum | solution.py:52
  84.9 2.8 copy-start
  87.7 4.3 copy-start.3
  94.3 366.3 %all-reduce.5.cloned.1.call-start = ((), (), s32[]{:S(2)}) async-start(), calls=%async_computation.3 | async-start | bytes 4718592 | tf_op jit(solution)/shard_map/psum | solution.py:52
  299.6 3.6 copy-start.23
  299.6 3.6 copy-start.27
  303.2 2.3 copy-start.8
  303.2 3.7 copy-start.9
  303.2 3.7 copy-start.26
  304.5 4.9 copy-start.14
  304.5 3.3 copy-start.24
  304.5 4.9 collective-permute-start
  307.7 4.1 copy-start.5
  307.8 4.1 collective-permute-start.2
  308.8 5.9 copy-start.1
  308.8 5.9 collective-permute-start.1
  313.2 3.4 copy-start.11
  460.6 3.2 copy-start.2
  460.6 3.5 copy-start.13
  464.1 4.5 copy-start.15
  464.1 4.5 copy-start.19
  464.1 4.5 copy-start.22
  465.2 48.0 %collective-permute-start.4 = (f32[432,1152]{1,0:T(8,128)S(1)}, f32[432,1152]{1,0:T(8,128)S(1)}, u32[]{:S(2)}, u32[]{:S(2)}) collective-permute-start(f32[432,1152]{1,0:T(8,128)S(1)} %fusion.1), channel_id=1, source_target_pairs={{0,32},{16,48},{32,0},{48,16},{64,96},{80,112},{96,64},{112,80},{1... | collective-permute-start | bytes 5971976 | tf_op jit(solution)/shard_map/ppermute | solution.py:15
  468.6 2.5 copy-start.6
  468.7 2.5 copy-start.7
  468.7 3.0 copy-start.10
  468.7 3.5 copy-start.17
  468.7 3.5 copy-start.21
  470.1 85.8 %collective-permute-start.3 = (f32[432,1152]{1,0:T(8,128)S(1)}, f32[432,1152]{1,0:T(8,128)S(1)}, u32[]{:S(2)}, u32[]{:S(2)}) collective-permute-start(f32[432,1152]{1,0:T(8,128)S(1)} %fusion.2), channel_id=1, source_target_pairs={{0,32},{16,48},{32,0},{48,16},{64,96},{80,112},{96,64},{112,80},{1... | collective-permute-start | bytes 5971976 | tf_op jit(solution)/shard_map/ppermute | solution.py:15
  473.1 115.2 %collective-permute-start.5 = (f32[432,1152]{1,0:T(8,128)S(1)}, f32[432,1152]{1,0:T(8,128)S(1)}, u32[]{:S(2)}, u32[]{:S(2)}) collective-permute-start(f32[432,1152]{1,0:T(8,128)S(1)} %fusion), channel_id=1, source_target_pairs={{0,32},{16,48},{32,0},{48,16},{64,96},{80,112},{96,64},{112,80},{1... | collective-permute-start | bytes 5971976 | tf_op jit(solution)/shard_map/ppermute | solution.py:15
  (6 other events, 7.7 us)
Sparse Core Ops, SparseCore 0:
  9.8 75.0 all-gather.2
  86.7 69.5 all-gather.4
  158.9 140.6 all-reduce.2
  319.8 140.7 all-reduce.4
where the time goes:
time: 597 us; the launch traced here: 596 us
  waiting for transfers between devices  537 us (90%)
  matrix products  26.8 us (4%)
  between operations  14 us (2%)
  starting transfers between devices  7.08 us (1%)
  local copies, waits for them, and re-layouts  6.79 us (1%)
    psum x2, waiting for transfers between devices, local(): output = lax.psum(partial_out, 'hid')  284 us
    ppermute x6, waiting for transfers between devices, swapped(): return lax.ppermute(value, axis, pairs)  113 us
    all_gather x1, waiting for transfers between devices, local(): lax.all_gather(tokens, 'hid', axis=1, tiled=True)  76.2 us
    all_gather x1, waiting for transfers between devices, local(): lax.all_gather(targets, 'hid', axis=1, tiled=True)  61.8 us
    dot_general x6, matrix products, contract_cols(): lax.dot_general(left, right, (((1,), (1,)), ((), ())), preferred_element_...  15.8 us
  transfers between devices with their start and end apart: 10, of which 9 were waited for; matrix products, arithmetic and copies ran while one was open for 3% of the time, Pallas kernels for 0%

commit v1 on v0

--- a/solution.py
+++ b/solution.py
@@ -2,11 +2,17 @@
 import jax.numpy as jnp
 from jax import lax
 from jax.sharding import PartitionSpec as P
+from jax.lax import all_gather
 
 D = 1152
 FF = 6912
 STEPS = 2
 LEARNING_RATE = 0.5
+
+
+def feed_blocks(block_in):
+    taken_in = jnp.sum(all_gather(block_in, axis_name="hid"), axis=0)
+    return taken_in
 
 
 def swapped(value, axis, distance):
@@ -49,7 +55,7 @@
         activated, gelu_back = jax.vjp(gelu_tanh, gate_value)
         hidden = (activated * up_value).astype(jnp.bfloat16)
         partial_out = jnp.dot(hidden, down_half, preferred_element_type=jnp.float32) * scale_hidden
-        output = lax.psum(partial_out, "hid")
+        output = feed_blocks(partial_out)
         residual = (output - all_targets[step_index].astype(jnp.float32)).astype(jnp.bfloat16)
         grad_down = contract_rows(hidden, residual) * scale_hidden
         hidden_grad = contract_cols(residual, down_half) * scale_hidden

time: 597 us -> 1130 us (1.89)
  waiting for transfers between devices: 537 us -> 1040 us
  other arithmetic: 4.99 us -> 34.2 us
    all_gather x0 -> x2, waiting for transfers between devices: none -> 786 us  [feed_blocks(): taken_in = jnp.sum(all_gather(block_in, axis_name='hid'), axis=0)]
    psum x2 -> x0, waiting for transfers between devices: 284 us -> none  [local(): output = lax.psum(partial_out, 'hid')]
    reduce_sum x0 -> x2, other arithmetic: none -> 29.2 us  [feed_blocks(): taken_in = jnp.sum(all_gather(block_in, axis_name='hid'), axis=0)]
  transfers between devices with their start and end apart: 10 -> 10, of which waited for: 9 -> 9; matrix products, arithmetic and copies ran while one was open for 3% -> 2% of each run, Pallas kernels for 0% -> 0%
where the time goes in v1:
time: 1130 us
  waiting for transfers between devices  1040 us (92%)
  other arithmetic  34.2 us (3%)
  matrix products  26.8 us (2%)
  between operations  14 us (1%)
    all_gather x2, waiting for transfers between devices, feed_blocks(): taken_in = jnp.sum(all_gather(block_in, axis_name='hid'), axis=0)  786 us
    ppermute x6, waiting for transfers between devices, swapped(): return lax.ppermute(value, axis, pairs)  122 us
    all_gather x1, waiting for transfers between devices, local(): lax.all_gather(tokens, 'hid', axis=1, tiled=True)  76.9 us
    all_gather x1, waiting for transfers between devices, local(): lax.all_gather(targets, 'hid', axis=1, tiled=True)  57 us
    reduce_sum x2, other arithmetic, feed_blocks(): taken_in = jnp.sum(all_gather(block_in, axis_name='hid'), axis=0)  29.2 us
  transfers between devices with their start and end apart: 10, of which 9 were waited for; matrix products, arithmetic and copies ran while one was open for 2% of the time, Pallas kernels for 0%

profile of v1, /device:TPU:2, one launch (start us, length us, event | category | flops | bytes accessed | tf_op | source)
XLA Modules:
  0.0 1132.0 jit_solution(12868495556848640955)
XLA Ops:
  7.9 76.9 %all-gather.7.cloned.1.call-done = bf16[2,512,1152]{2,1,0:T(8,128)(2,1)} async-done(((bf16[2,32,1152]{2,1,0:T(8,128)(2,1)}), bf16[2,512,1152]{2,1,0:T(8,128)(2,1)}) %all-gather.7.cloned.1.call-update) | async-done | bytes 2359312 | tf_op jit(solution)/shard_map/all_gather | solution.py:44
  84.9 2.8 convolution_multiply_fusion.13
  87.7 3.5 multiply_convert_fusion.3
  92.0 2.3 convolution_multiply_fusion.1
  95.1 392.7 %all-gather.11.cloned.1.call-done = f32[8192,1152]{1,0:T(8,128)} async-done(((f32[512,1152]{1,0:T(8,128)}), f32[8192,1152]{1,0:T(8,128)}) %all-gather.11.cloned.1.call-update) | async-done | bytes 37748752 | tf_op jit(solution)/shard_map/all_gather | solution.py:14
  487.8 14.6 %reduce_sum.20 = f32[512,1152]{1,0:T(8,128)} reduce(f32[16,512,1152]{2,1,0:T(8,128)} %bitcast.84, f32[]{:T(128)} %constant.26.clone.1), dimensions={0}, to_apply=%region_0.0 | reduce | flops 8847360 | bytes 40108036 | tf_op jit(solution)/shard_map/reduce_sum | solution.py:14
  502.4 57.0 %all-gather.9.cloned.1.call-done = bf16[2,512,1152]{2,1,0:T(8,128)(2,1)} async-done(((bf16[2,32,1152]{2,1,0:T(8,128)(2,1)}), bf16[2,512,1152]{2,1,0:T(8,128)(2,1)}) %all-gather.9.cloned.1.call-update) | async-done | bytes 2359312 | tf_op jit(solution)/shard_map/all_gather | solution.py:45
  559.4 3.5 convolution_multiply_fusion.11
  563.0 1.3 fusion.5
  565.2 1.4 copy-done.9
  566.7 0.9 fusion.3
  567.7 1.0 fusion.4
  570.7 1.0 collective-permute-done.2
  572.0 1.0 copy-done.16
  573.0 1.5 collective-permute-done.1
  574.5 1.9 multiply_convert_fusion.1
  577.2 2.3 convolution_multiply_fusion
  579.5 393.4 %all-gather.13.cloned.1.call-done = f32[8192,1152]{1,0:T(8,128)} async-done(((f32[512,1152]{1,0:T(8,128)}), f32[8192,1152]{1,0:T(8,128)}) %all-gather.13.cloned.1.call-update) | async-done | bytes 37748752 | tf_op jit(solution)/shard_map/all_gather | solution.py:14
  973.0 14.6 %reduce_sum.22 = f32[512,1152]{1,0:T(8,128)} reduce(f32[16,512,1152]{2,1,0:T(8,128)} %bitcast.85, f32[]{:T(128)} %constant.26.clone.1), dimensions={0}, to_apply=%region_1.0 | reduce | flops 8847360 | bytes 40108036 | tf_op jit(solution)/shard_map/reduce_sum | solution.py:14
  987.6 3.2 convolution_multiply_fusion.8
  991.1 1.0 fusion.1
  992.1 2.8 collective-permute-start.4
  995.0 1.4 fusion.2
  996.3 1.3 collective-permute-start.3
  998.5 0.9 fusion
  999.4 1.6 collective-permute-start.5
  1001.0 38.9 %collective-permute-done.4 = f32[432,1152]{1,0:T(8,128)S(1)} collective-permute-done((f32[432,1152]{1,0:T(8,128)S(1)}, f32[432,1152]{1,0:T(8,128)S(1)}, u32[]{:S(2)}, u32[]{:S(2)}) %collective-permute-start.4) | collective-permute-done | bytes 1990688 | tf_op jit(solution)/shard_map/ppermute | solution.py:21
  1039.9 1.6 multiply_bitcast_fusion.1
  1041.5 41.1 %collective-permute-done.3 = f32[432,1152]{1,0:T(8,128)S(1)} collective-permute-done((f32[432,1152]{1,0:T(8,128)S(1)}, f32[432,1152]{1,0:T(8,128)S(1)}, u32[]{:S(2)}, u32[]{:S(2)}) %collective-permute-start.3) | collective-permute-done | bytes 1990688 | tf_op jit(solution)/shard_map/ppermute | solution.py:21
  1082.6 1.6 multiply_bitcast_fusion.2
  1084.2 39.8 %collective-permute-done.5 = f32[432,1152]{1,0:T(8,128)S(1)} collective-permute-done((f32[432,1152]{1,0:T(8,128)S(1)}, f32[432,1152]{1,0:T(8,128)S(1)}, u32[]{:S(2)}, u32[]{:S(2)}) %collective-permute-start.5) | collective-permute-done | bytes 1990688 | tf_op jit(solution)/shard_map/ppermute | solution.py:21
  1124.0 1.6 multiply_bitcast_fusion
  (68 shorter events, 7.7 us)
Async XLA Ops:
  7.2 77.7 %all-gather.7.cloned.1.call-start = ((), (), s32[]{:S(2)}) async-start(), calls=%async_computation | async-start | bytes 2506752 | tf_op jit(solution)/shard_map/all_gather | solution.py:44
  7.9 479.9 %all-gather.11.cloned.1.call-start = ((), (), s32[]{:S(2)}) async-start(), calls=%async_computation.2 | async-start | bytes 40108032 | tf_op jit(solution)/shard_map/all_gather | solution.py:14
  84.9 2.8 copy-start
  87.7 4.3 copy-start.5
  94.3 465.1 %all-gather.9.cloned.1.call-start = ((), (), s32[]{:S(2)}) async-start(), calls=%async_computation.1 | async-start | bytes 2506752 | tf_op jit(solution)/shard_map/all_gather | solution.py:45
  95.1 877.9 %all-gather.13.cloned.1.call-start = ((), (), s32[]{:S(2)}) async-start(), calls=%async_computation.3 | async-start | bytes 40108032 | tf_op jit(solution)/shard_map/all_gather | solution.py:14
  559.4 3.6 copy-start.23
  559.4 3.6 copy-start.27
  563.0 2.3 copy-start.6
  563.0 3.7 copy-start.9
  563.0 3.7 copy-start.26
  564.3 5.1 copy-start.14
  564.3 3.3 copy-start.24
  564.3 5.1 collective-permute-start
  567.5 4.1 copy-start.7
  567.6 4.1 collective-permute-start.2
  568.6 5.9 copy-start.3
  568.6 5.9 collective-permute-start.1
  573.0 3.5 copy-start.11
  987.6 3.2 copy-start.4
  987.6 3.5 copy-start.13
  991.1 3.8 copy-start.15
  991.1 3.8 copy-start.19
  991.1 3.8 copy-start.22
  992.1 47.8 %collective-permute-start.4 = (f32[432,1152]{1,0:T(8,128)S(1)}, f32[432,1152]{1,0:T(8,128)S(1)}, u32[]{:S(2)}, u32[]{:S(2)}) collective-permute-start(f32[432,1152]{1,0:T(8,128)S(1)} %fusion.1), channel_id=1, source_target_pairs={{0,32},{16,48},{32,0},{48,16},{64,96},{80,112},{96,64},{112,80},{1... | collective-permute-start | bytes 5971976 | tf_op jit(solution)/shard_map/ppermute | solution.py:21
  994.9 2.7 copy-start.1
  994.9 2.7 copy-start.8
  995.0 3.0 copy-start.10
  995.0 3.5 copy-start.17
  995.0 3.5 copy-start.21
  996.3 86.2 %collective-permute-start.3 = (f32[432,1152]{1,0:T(8,128)S(1)}, f32[432,1152]{1,0:T(8,128)S(1)}, u32[]{:S(2)}, u32[]{:S(2)}) collective-permute-start(f32[432,1152]{1,0:T(8,128)S(1)} %fusion.2), channel_id=1, source_target_pairs={{0,32},{16,48},{32,0},{48,16},{64,96},{80,112},{96,64},{112,80},{1... | collective-permute-start | bytes 5971976 | tf_op jit(solution)/shard_map/ppermute | solution.py:21
  999.4 124.5 %collective-permute-start.5 = (f32[432,1152]{1,0:T(8,128)S(1)}, f32[432,1152]{1,0:T(8,128)S(1)}, u32[]{:S(2)}, u32[]{:S(2)}) collective-permute-start(f32[432,1152]{1,0:T(8,128)S(1)} %fusion), channel_id=1, source_target_pairs={{0,32},{16,48},{32,0},{48,16},{64,96},{80,112},{96,64},{112,80},{1... | collective-permute-start | bytes 5971976 | tf_op jit(solution)/shard_map/ppermute | solution.py:21
  (6 other events, 7.7 us)
Sparse Core Ops, SparseCore 0:
  9.8 75.0 all-gather.6
  94.5 393.2 all-gather.10
  489.6 69.7 all-gather.8
  579.6 393.2 all-gather.12
